TPU v7x, 32 devices: a whole 2x2x4 slice. The times are simulated.
32 devices in a mesh: item: 8 (over y, x, core), dp: 4 (over z).
Axes of the slice: x: 2, y: 2, z: 4, core: 2. Of those that a mesh axis runs over, the one named last changes fastest.
Arguments:
- hidden_states: bfloat16 [32768, 512], P(('item', 'dp'))
- item_table: bfloat16 [4096, 512], P('item'), may hold values from -0.25 to 0.25
- cand_local: int32 [64], replicated, may hold values from 0 to 511
- log_sample: float32 [64], replicated, may hold values from -14 to -4
- target_slot: int32 [32768], P(('item', 'dp')), may hold values from 0 to 63
- loss_weight: float32 [32768], P(('item', 'dp')), may hold values from -6 to 6
Outputs:
- grad_hidden: bfloat16 [32768, 512], P(('item', 'dp'))
- grad_table: float32 [4096, 512], P('item')
Inputs may be any that keep to these rules, and one draw needn't show every extreme that they name: Candidate slot s belongs to the item shard s // 8; cand_local counts rows within that shard, and a row may be sampled more than once.
All inputs are finite; a program needn't handle non-finite values.
Results may differ from a plain program's by a relative error of at most 0.0049.
Values may be sent and summed in bfloat16 or wider, within the bound.
No kernel may reach another device: no remote copies, remote signals or barrier semaphores. Data moves between devices by JAX's collectives and lax.ppermute only.
A program may use at most 64 MiB of HBM per device.

v0:
```python
import math

import jax
import jax.numpy as jnp
from jax import lax
from jax.sharding import PartitionSpec as P


def on_device(hidden_states, item_table, cand_local, log_sample, target_slot, loss_weight):
    owners = lax.axis_size("item")
    total_cands = log_sample.shape[0]
    per_owner = total_cands // owners
    my_index = lax.axis_index("item")
    my_local = lax.dynamic_slice_in_dim(cand_local, my_index * per_owner, per_owner)
    my_rows = item_table[my_local]
    cand_rows = lax.all_gather(my_rows, "item", axis=0, tiled=True)
    slots = jnp.arange(total_cands, dtype=jnp.int32)
    tok_rows = hidden_states.shape[0]
    width = hidden_states.shape[1]
    block = math.gcd(tok_rows, 512)
    count = tok_rows // block
    states = hidden_states.reshape(count, block, width)
    targets = target_slot.reshape(count, block)
    weights = loss_weight.reshape(count, block)

    def step(total, inputs):
        rows, tgt, wts = inputs
        logits = (
            jnp.dot(rows, cand_rows.T, preferred_element_type=jnp.float32) - log_sample[None, :]
        )
        probs = jax.nn.softmax(logits, axis=1)
        onehot = (tgt[:, None] == slots[None, :]).astype(jnp.float32)
        grad_logits = (wts[:, None] * (probs - onehot)).astype(jnp.bfloat16)
        grad_rows = jnp.dot(grad_logits, cand_rows, preferred_element_type=jnp.float32).astype(
            jnp.bfloat16
        )
        total = total + jnp.dot(grad_logits.T, rows, preferred_element_type=jnp.float32)
        return (total, grad_rows)

    partial_grad, grad_blocks = lax.scan(
        step, jnp.zeros((total_cands, width), jnp.float32), (states, targets, weights)
    )
    grad_hidden = grad_blocks.reshape(tok_rows, width)
    owned = lax.psum_scatter(partial_grad, "item", scatter_dimension=0, tiled=True)
    owned = lax.psum(owned, "dp")
    table_rows = item_table.shape[0]
    placing = (my_local[:, None] == jnp.arange(table_rows, dtype=jnp.int32)[None, :]).astype(
        jnp.float32
    )
    grad_table = jnp.dot(
        placing.T, owned, preferred_element_type=jnp.float32, precision=lax.Precision.HIGHEST
    )
    return (grad_hidden, grad_table)


def solution(mesh):
    placed = (
        P(("item", "dp"), None),
        P("item", None),
        P(),
        P(),
        P(("item", "dp")),
        P(("item", "dp")),
    )
    return jax.shard_map(
        on_device,
        mesh=mesh,
        in_specs=placed,
        out_specs=(P(("item", "dp"), None), P("item", None)),
        check_vma=False,
    )
```

profile of v0, /device:TPU:0, one launch (start us, length us, event | category | flops | bytes accessed | tf_op | source)
XLA Modules:
  0.0 87.7 jit_solution(3988291975070287816)
XLA Ops:
  7.2 0.0 copy-start
  7.2 0.0 reduce-scatter.2.cloned.1.call-start
  7.3 0.0 copy-start.6
  7.3 0.7 copy-done.6
  8.0 0.1 compare_select_fusion
  8.0 0.2 copy-done
  8.2 0.6 gather_fusion
  8.8 0.0 copy-start.4
  8.8 10.7 %all-gather = bf16[64,512]{1,0:T(8,128)(2,1)S(1)} all-gather(bf16[8,512]{1,0:T(8,128)(2,1)S(1)} %gather_fusion), channel_id=2, replica_groups=mesh['item'=8,'dp'=4] {'item'}, dimensions={0}, use_global_device_ids=true | all-gather | bytes 73728 | tf_op jit(solution)/shard_map/all_gather | solution.py:16
  19.5 0.0 copy-done.4
  19.5 0.0 copy-start.5
  19.6 0.7 copy-done.5
  20.2 0.0 copy-start.3
  20.2 0.7 copy-done.3
  20.9 4.2 %while.13 = (s32[]{:T(128)}, f32[64,512]{1,0:T(8,128)S(1)}, bf16[2,512,512]{2,1,0:T(8,128)(2,1)S(1)}, f32[2,512]{1,0:T(2,128)S(1)}, bf16[2,512,512]{2,1,0:T(8,12...) while((s32[]{:T(128)}, f32[64,512]{1,0:T(8,128)S(1)}, ...), condition=%wide.region_3.4_spmd.clone, body=%wide.region_0.3_spmd.clone.sunk | while | flops 101579776 | bytes 6716315 | solution.py:40
  20.9 0.0 copy-start.1
  20.9 1.4 %fusion.26 = (f32[512]{0:T(512)S(1)}, f32[512,64]{0,1:T(8,128)S(1)}) fusion(f32[64]{0:T(128)S(1)} %get-tuple-element.180, bf16[64,512]{1,0:T(8,128)(2,1)S(1)} %get-tuple-element.179, bf16[2,512,512]{2,1,0:T(8,128)(2,1)} %get-tuple-element.178, s32[]{:T(128)} %get-tuple-element.164), kind=kOutput, calls=%fused_computation.24.clone.1 | convolution fusion | flops 33619456 | bytes 723712 | tf_op jit(solution)/shard_map/while/body/eval_jaxpr/dot_general | solution.py:29
  22.4 0.3 fusion.28
  22.8 0.0 copy-done.1
  22.8 0.2 convolution_add_fusion.2
  23.0 0.0 copy-start.1
  23.0 1.4 %fusion.26 = (f32[512]{0:T(512)S(1)}, f32[512,64]{0,1:T(8,128)S(1)}) fusion(f32[64]{0:T(128)S(1)} %get-tuple-element.180, bf16[64,512]{1,0:T(8,128)(2,1)S(1)} %get-tuple-element.179, bf16[2,512,512]{2,1,0:T(8,128)(2,1)} %get-tuple-element.178, s32[]{:T(128)} %get-tuple-element.164), kind=kOutput, calls=%fused_computation.24.clone.1 | convolution fusion | flops 33619456 | bytes 723712 | tf_op jit(solution)/shard_map/while/body/eval_jaxpr/dot_general | solution.py:29
  24.5 0.3 fusion.28
  24.9 0.0 copy-done.1
  24.9 0.2 convolution_add_fusion.2
  25.1 0.0 copy-start.2
  25.2 0.0 copy-start.7
  25.2 0.6 copy-done.2
  25.8 0.0 reduce-scatter.2.cloned.1.call-update
  25.8 34.0 %reduce-scatter.2.cloned.1.call-done = f32[8,512]{1,0:T(8,128)} async-done(((f32[64,512]{1,0:T(8,128)}), f32[8,512]{1,0:T(8,128)}) %reduce-scatter.2.cloned.1.call-update) | async-done | bytes 16400 | tf_op jit(solution)/shard_map/reduce_scatter | solution.py:44
  59.8 19.4 %psum.7 = f32[8,512]{1,0:T(8,128)S(1)} all-reduce(f32[8,512]{1,0:T(8,128)} %reduce-scatter.2.cloned.1.call-done), channel_id=1, replica_groups=mesh['item'=8,'dp'=4] {'dp'}, use_global_device_ids=true, to_apply=%region_5.6 | all-reduce | flops 4096 | bytes 32768 | tf_op jit(solution)/shard_map/psum | solution.py:45
  79.2 1.7 %fusion.11 = f32[512,512]{1,0:T(8,128)} fusion(f32[8,512]{1,0:T(8,128)S(1)} %psum.7, s32[8]{0:T(128)S(1)} %get-tuple-element.98), kind=kOutput, calls=%fused_computation.20 | convolution fusion | flops 25169920 | bytes 1064992 | tf_op jit(solution)/shard_map/dot_general | solution.py:50
  80.8 0.0 copy-done.7
  (11 shorter events, 0.2 us)
Async XLA Ops:
  7.2 1.1 %copy-start = (bf16[512,512]{1,0:T(8,128)(2,1)S(1)}, bf16[512,512]{1,0:T(8,128)(2,1)}, u32[]{:S(2)}) copy-start(bf16[512,512]{1,0:T(8,128)(2,1)} %param.9) | copy-start | bytes 1572868
  7.2 52.6 %reduce-scatter.2.cloned.1.call-start = ((), (), s32[]{:S(2)}) async-start(), calls=%async_computation.1 | async-start | bytes 147456 | tf_op jit(solution)/shard_map/reduce_scatter | solution.py:44
  7.3 0.7 copy-start.6
  8.8 10.7 %copy-start.4 = (f32[1024]{0:T(1024)S(1)}, f32[1024]{0:T(1024)}, u32[]{:S(2)}) copy-start(f32[1024]{0:T(1024)} %param.13) | copy-start | bytes 12292
  19.5 0.7 copy-start.5
  20.2 0.7 copy-start.3
  20.9 1.9 %copy-start.1 = (bf16[2,512,512]{2,1,0:T(8,128)(2,1)S(1)}, bf16[2,512,512]{2,1,0:T(8,128)(2,1)}, u32[]{:S(2)}) copy-start(bf16[2,512,512]{2,1,0:T(8,128)(2,1)} %get-tuple-element.178) | copy-start | bytes 3145732 | tf_op jit(solution)/shard_map/while
  23.0 1.9 %copy-start.1 = (bf16[2,512,512]{2,1,0:T(8,128)(2,1)S(1)}, bf16[2,512,512]{2,1,0:T(8,128)(2,1)}, u32[]{:S(2)}) copy-start(bf16[2,512,512]{2,1,0:T(8,128)(2,1)} %get-tuple-element.178) | copy-start | bytes 3145732 | tf_op jit(solution)/shard_map/while
  25.1 0.7 copy-start.2
  25.2 55.7 %copy-start.7 = (bf16[2,512,512]{2,1,0:T(8,128)(2,1)}, bf16[2,512,512]{2,1,0:T(8,128)(2,1)S(1)}, u32[]{:S(2)}) copy-start(bf16[2,512,512]{2,1,0:T(8,128)(2,1)S(1)} %get-tuple-element.50) | copy-start | bytes 3145732
Sparse Core Ops, SparseCore 0:
  26.0 33.8 reduce-scatter.1
where the time goes:
time: 88 us; the launch traced here: 87.7 us
  waiting for transfers between devices  34 us (39%)
  blocking collectives  30.1 us (34%)
  between operations  14.1 us (16%)
  matrix products  5.64 us (6%)
  local copies, waits for them, and re-layouts  3.5 us (4%)
    reduce_scatter x1, waiting for transfers between devices, on_device(): lax.psum_scatter(partial_grad, 'item', scatter_dimension=0, tiled=True)  34 us
    psum x1, blocking collectives, on_device(): owned = lax.psum(owned, 'dp')  19.4 us
    all_gather x1, blocking collectives, on_device(): cand_rows = lax.all_gather(my_rows, 'item', axis=0, tiled=True)  10.7 us
    unnamed x14, local copies, waits for them, and re-layouts  2.87 us
    dot_general x2, matrix products, step(): jnp.dot(rows, cand_rows.T, preferred_element_type=jnp.float32)  2.86 us
  transfers between devices with their start and end apart: 1, of which 1 were waited for; matrix products, arithmetic and copies ran while one was open for 0% of the time, Pallas kernels for 0%

commit v1 on v0

v1 whole, which is shorter than its diff:
```python
import jax
import jax.numpy as jnp
from jax import lax
from jax.sharding import PartitionSpec as P

AXES = ("item", "dp")


def exchange(value, axis, mask):
    size = lax.axis_size(axis)
    return lax.ppermute(value, axis, [(i, i ^ mask) for i in range(size)])


def levels_of(size):
    levels, bit = [], 2
    while bit < size:
        if 2 * bit < size:
            levels.append((bit ^ 1, (2 * bit) ^ 1, (3 * bit) ^ 1))
            bit *= 4
        else:
            levels.append((bit ^ 1,))
            bit *= 2
    return levels


def gather_rows(mine):
    size = lax.axis_size("item")
    blocks = {0: mine}
    if size > 1:
        blocks[1] = exchange(mine, "item", 1)
    for masks in levels_of(size):
        held = sorted(blocks)
        fresh = {}
        for mask in masks[::-1]:
            order = sorted(held, key=lambda k: k ^ mask)
            got = exchange(jnp.concatenate([blocks[k] for k in order]), "item", mask)
            for place, piece in zip(order, jnp.split(got, len(order))):
                fresh[place ^ mask] = piece
        blocks.update(fresh)
    return jnp.concatenate([blocks[k] for k in range(size)])


def scatter_sum(blocks):
    size = lax.axis_size("item")
    levels = ([(1,)] if size > 1 else []) + levels_of(size)
    kept = [{0}]
    for masks in levels[::-1]:
        kept.append({mask ^ k for mask in (0,) + masks for k in kept[-1]})
    kept = kept[::-1]
    assert len(kept[0]) == size
    for masks, rest in zip(levels, kept[1:]):
        order = sorted(rest)
        got = []
        for mask in masks[::-1]:
            out = jnp.concatenate([blocks[k ^ mask] for k in order]).astype(jnp.bfloat16)
            got.append(exchange(out, "item", mask))
        sums = {}
        for place, k in enumerate(order):
            total = blocks[k]
            for piece in got:
                step = piece.shape[0] // len(order)
                total = total + piece[place * step : (place + 1) * step].astype(jnp.float32)
            sums[k] = total
        blocks = sums
    return blocks[0]


def batch_sum(value):
    size = lax.axis_size("dp")
    bit = 1
    while bit < size:
        mine = value.astype(jnp.bfloat16)
        if 2 * bit < size:
            far = exchange(mine, "dp", 3 * bit)
            mid = exchange(mine, "dp", 2 * bit)
            near = exchange(mine, "dp", bit)
            wide = [v.astype(jnp.float32) for v in (mine, near, mid, far)]
            value = (wide[0] + wide[1]) + (wide[2] + wide[3])
            bit *= 4
        else:
            other = exchange(mine, "dp", bit)
            value = mine.astype(jnp.float32) + other.astype(jnp.float32)
            bit *= 2
    return value


def on_device(hidden_states, item_table, cand_local, log_sample, target_slot, loss_weight):
    owners = lax.axis_size("item")
    total_cands = log_sample.shape[0]
    per_owner = total_cands // owners
    my_index = lax.axis_index("item")
    my_local = lax.dynamic_slice_in_dim(cand_local, my_index * per_owner, per_owner)
    table_rows = item_table.shape[0]
    my_rows = item_table[my_local]
    cand_rows = gather_rows(my_rows)
    place = jnp.arange(total_cands, dtype=jnp.int32)
    slots = ((place // per_owner) ^ my_index) * per_owner + place % per_owner
    log_q = log_sample[slots]
    logits = jnp.dot(cand_rows, hidden_states.T, preferred_element_type=jnp.float32) - log_q[:, None]
    probs = jax.nn.softmax(logits, axis=0)
    onehot = (target_slot[None, :] == slots[:, None]).astype(jnp.float32)
    grad_logits = (loss_weight[None, :] * (probs - onehot)).astype(jnp.bfloat16)
    partial = jnp.dot(grad_logits, hidden_states, preferred_element_type=jnp.float32)
    grad_hidden = jnp.dot(grad_logits.T, cand_rows, preferred_element_type=jnp.float32).astype(
        jnp.bfloat16
    )
    terms = {k: partial[k * per_owner : (k + 1) * per_owner] for k in range(owners)}
    owned = batch_sum(scatter_sum(terms))
    placing = (my_local[:, None] == jnp.arange(table_rows, dtype=jnp.int32)[None, :]).astype(
        jnp.float32
    )
    grad_table = jnp.dot(
        placing.T, owned, preferred_element_type=jnp.float32, precision=lax.Precision.HIGHEST
    )
    return (grad_hidden, grad_table)


def solution(mesh):
    placed = (
        P(AXES, None),
        P("item", None),
        P(),
        P(),
        P(AXES),
        P(AXES),
    )
    return jax.shard_map(
        on_device,
        mesh=mesh,
        in_specs=placed,
        out_specs=(P(AXES, None), P("item", None)),
        check_vma=False,
    )
```

time: 88 us -> 30.5 us (0.35)
  blocking collectives: 30.1 us -> 0 us
  waiting for transfers between devices: 34 us -> 8.77 us
  between operations: 14.1 us -> 0.79 us
  starting transfers between devices: 0.04 us -> 12.7 us
  matrix products: 5.64 us -> 3.95 us
    reduce_scatter x1 -> x0, waiting for transfers between devices: 34 us -> none  [on_device(): lax.psum_scatter(partial_grad, 'item', scatter_dimension=0, tiled=True)]
    psum x1 -> x0, blocking collectives: 19.4 us -> none  [on_device(): owned = lax.psum(owned, 'dp')]
    ppermute x0 -> x11, starting transfers between devices: none -> 12.7 us  [exchange(): return lax.ppermute(value, axis, [(i, i ^ mask) for i in range(size)])]
    all_gather x1 -> x0, blocking collectives: 10.7 us -> none  [on_device(): cand_rows = lax.all_gather(my_rows, 'item', axis=0, tiled=True)]
    ppermute x0 -> x11, waiting for transfers between devices: none -> 8.77 us  [exchange(): return lax.ppermute(value, axis, [(i, i ^ mask) for i in range(size)])]
    unnamed x14 -> x10, local copies, waits for them, and re-layouts: 2.87 us -> 0.03 us
    dot_general x6 -> x3, matrix products: 3.98 us -> 2.29 us  [the longest x1 1.5 us: on_device(): jnp.dot(grad_logits.T, cand_rows, preferred_element_type=jnp.float32)]
    gather x0 -> x1, local copies, waits for them, and re-layouts: none -> 1.44 us  [on_device(): log_q = log_sample[slots]]
  transfers between devices with their start and end apart: 1 -> 11, of which waited for: 1 -> 6; matrix products, arithmetic and copies ran while one was open for 0% -> 10% of each run, Pallas kernels for 0% -> 0%
where the time goes in v1:
time: 30.5 us; the launch traced here: 30.3 us
  starting transfers between devices  12.7 us (42%)
  waiting for transfers between devices  8.77 us (29%)
  matrix products  3.95 us (13%)
  local copies, waits for them, and re-layouts  3.16 us (10%)
  other arithmetic  0.93 us (3%)
  between operations  0.79 us (3%)
    ppermute x11, starting transfers between devices, exchange(): return lax.ppermute(value, axis, [(i, i ^ mask) for i in range(size)])  12.7 us
    ppermute x11, waiting for transfers between devices, exchange(): return lax.ppermute(value, axis, [(i, i ^ mask) for i in range(size)])  8.77 us
    gather x1, local copies, waits for them, and re-layouts, on_device(): my_rows = item_table[my_local]  1.68 us
    dot_general x1, matrix products, on_device(): jnp.dot(placing.T, owned, preferred_element_type=jnp.float32, precision=l...  1.66 us
    dot_general x1, matrix products, on_device(): jnp.dot(grad_logits.T, cand_rows, preferred_element_type=jnp.float32)  1.5 us
    gather x1, local copies, waits for them, and re-layouts, on_device(): log_q = log_sample[slots]  1.44 us
    select_n x1, other arithmetic, on_device(): my_rows = item_table[my_local]  0.82 us
  transfers between devices with their start and end apart: 11, of which 6 were waited for; matrix products, arithmetic and copies ran while one was open for 10% of the time, Pallas kernels for 0%

profile of v1, /device:TPU:0, one launch (start us, length us, event | category | flops | bytes accessed | tf_op | source)
XLA Modules:
  0.0 30.3 jit_solution(14170348644227674345)
XLA Ops:
  0.6 0.0 copy-start
  0.6 0.8 %compare_select_fusion.1 = (s32[8]{0:T(128)S(1)}, s32[8]{0:T(128)S(1)}) fusion(s32[64]{0:T(128)} %param.8, s32[]{:T(128)S(6)} %select_n.52), kind=kLoop, calls=%fused_computation.39 | loop fusion | flops 24 | bytes 100 | tf_op jit(solution)/shard_map/select_n | solution.py:94
  1.5 1.7 %gather_fusion = bf16[8,512]{1,0:T(8,128)(2,1)S(1)} fusion(bf16[512,512]{1,0:T(8,128)(2,1)} %param.7, s32[1024]{0:T(1024)S(1)} %pad_clamp_fusion.1), kind=kCustom, calls=%fused_computation | custom fusion | bytes 16416 | tf_op jit(solution)/shard_map/gather | solution.py:94
  3.2 0.6 %collective-permute-start = (bf16[8,512]{1,0:T(8,128)(2,1)S(1)}, bf16[8,512]{1,0:T(8,128)(2,1)S(1)}, u32[]{:S(2)}, u32[]{:S(2)}) collective-permute-start(bf16[8,512]{1,0:T(8,128)(2,1)S(1)} %gather_fusion), channel_id=1, source_target_pairs={{0,4},{4,0},{8,12},{12,8},{16,20},{20,16},{24,28},{28,24},{1,5},{5... | collective-permute-start | bytes 24584 | tf_op jit(solution)/shard_map/ppermute | solution.py:11
  3.8 0.0 copy-start.1
  3.8 0.0 copy-start.2
  3.8 1.4 %gather_fusion.1 = f32[64]{0:T(128)S(1)} fusion(f32[64]{0:T(128)} %param.9, s32[1024]{0:T(1024)S(1)} %pad_clamp_fusion), kind=kCustom, calls=%fused_computation.1 | custom fusion | bytes 768 | tf_op jit(solution)/shard_map/gather | solution.py:98
  5.2 0.0 collective-permute-done
  5.2 3.6 %collective-permute-start.3 = (bf16[16,512]{1,0:T(8,128)(2,1)S(1)}, bf16[16,512]{1,0:T(8,128)(2,1)S(1)}, u32[]{:S(2)}, u32[]{:S(2)}) collective-permute-start(bf16[16,512]{1,0:T(8,128)(2,1)S(1)} %get-tuple-element.9), channel_id=1, source_target_pairs={{0,28},{4,24},{8,20},{12,16},{16,12},{20,8},{24,4},{28,0},{1,29},{... | collective-permute-start | bytes 49160 | tf_op jit(solution)/shard_map/ppermute | solution.py:11
  8.9 0.1 collective-permute-start.2
  9.0 0.1 collective-permute-start.1
  9.1 3.0 %collective-permute-done.1 = bf16[16,512]{1,0:T(8,128)(2,1)S(1)} collective-permute-done((bf16[16,512]{1,0:T(8,128)(2,1)S(1)}, bf16[16,512]{1,0:T(8,128)(2,1)S(1)}, u32[]{:S(2)}, u32[]{:S(2)}) %collective-permute-start.1) | collective-permute-done | bytes 16416 | tf_op jit(solution)/shard_map/ppermute | solution.py:11
  12.2 0.0 collective-permute-done.2
  12.2 0.0 collective-permute-done.3
  12.2 0.0 copy-done
  12.2 0.4 %fusion.26 = (f32[1024]{0:T(1024)S(1)}, f32[64,1024]{1,0:T(8,128)S(1)}) fusion(f32[64]{0:T(128)S(1)} %gather_fusion.1, bf16[64,512]{1,0:T(8,128)(2,1)S(1)} %constant_dynamic-update-slice_fusion.2, bf16[1024,512]{1,0:T(8,128)(2,1)S(1)} %copy-done), kind=kOutput, calls=%fused_computation.59 | convolution fusion | flops 67238912 | bytes 1380608 | tf_op jit(solution)/shard_map/dot_general | solution.py:99
  12.7 0.1 fusion
  12.7 0.0 copy-done.1
  12.7 0.0 copy-done.2
  12.7 0.3 %fusion.27 = (bf16[64,512]{1,0:T(8,128)(2,1)S(1)}, f32[64,512]{1,0:T(8,128)S(1)}) fusion(bf16[1024,512]{1,0:T(8,128)(2,1)S(1)} %copy-done, f32[64,1024]{1,0:T(8,128)S(1)} %get-tuple-element.12, s32[1024]{0:T(1024)S(1)} %copy-done.1, f32[1024]{0:T(1024)S(1)} %fusion, f32[1024]{0:T(1024)S(1)} %get-tuple-element.11, f32[1024]{0:T(1024)S(1)} %copy-done.2, ...), kind=kOutput, calls=%fused_computation.60 | convolution fusion | flops 67600384 | bytes 1523968 | tf_op jit(solution)/shard_map/dot_general | solution.py:103
  13.1 0.6 %collective-permute-start.4 = (bf16[32,512]{1,0:T(8,128)(2,1)S(1)}, bf16[32,512]{1,0:T(8,128)(2,1)S(1)}, u32[]{:S(2)}, u32[]{:S(2)}) collective-permute-start(bf16[32,512]{1,0:T(8,128)(2,1)S(1)} %pad_maximum_fusion), channel_id=1, source_target_pairs={{0,4},{4,0},{8,12},{12,8},{16,20},{20,16},{24,28},{28,24},{1,5},{5... | collective-permute-start | bytes 98312 | tf_op jit(solution)/shard_map/ppermute | solution.py:11
  13.7 0.9 %collective-permute-done.4 = bf16[32,512]{1,0:T(8,128)(2,1)S(1)} collective-permute-done((bf16[32,512]{1,0:T(8,128)(2,1)S(1)}, bf16[32,512]{1,0:T(8,128)(2,1)S(1)}, u32[]{:S(2)}, u32[]{:S(2)}) %collective-permute-start.4) | collective-permute-done | bytes 32800 | tf_op jit(solution)/shard_map/ppermute | solution.py:11
  14.5 1.5 %collective-permute-start.5 = (bf16[8,512]{1,0:T(8,128)(2,1)S(1)}, bf16[8,512]{1,0:T(8,128)(2,1)S(1)}, u32[]{:S(2)}, u32[]{:S(2)}) collective-permute-start(bf16[8,512]{1,0:T(8,128)(2,1)S(1)} %get-tuple-element.4), channel_id=1, source_target_pairs={{0,28},{4,24},{8,20},{12,16},{16,12},{20,8},{24,4},{28,0},{1,29},{... | collective-permute-start | bytes 24584 | tf_op jit(solution)/shard_map/ppermute | solution.py:11
  16.1 1.3 %collective-permute-start.7 = (bf16[8,512]{1,0:T(8,128)(2,1)S(1)}, bf16[8,512]{1,0:T(8,128)(2,1)S(1)}, u32[]{:S(2)}, u32[]{:S(2)}) collective-permute-start(bf16[8,512]{1,0:T(8,128)(2,1)S(1)} %get-tuple-element.5), channel_id=1, source_target_pairs={{0,12},{4,8},{8,4},{12,0},{16,28},{20,24},{24,20},{28,16},{1,13},{... | collective-permute-start | bytes 24584 | tf_op jit(solution)/shard_map/ppermute | solution.py:11
  17.3 0.5 %collective-permute-start.6 = (bf16[8,512]{1,0:T(8,128)(2,1)S(1)}, bf16[8,512]{1,0:T(8,128)(2,1)S(1)}, u32[]{:S(2)}, u32[]{:S(2)}) collective-permute-start(bf16[8,512]{1,0:T(8,128)(2,1)S(1)} %get-tuple-element.6), channel_id=1, source_target_pairs={{0,20},{4,16},{8,28},{12,24},{16,4},{20,0},{24,12},{28,8},{1,21},{... | collective-permute-start | bytes 24584 | tf_op jit(solution)/shard_map/ppermute | solution.py:11
  17.8 0.8 %collective-permute-done.5 = bf16[8,512]{1,0:T(8,128)(2,1)S(1)} collective-permute-done((bf16[8,512]{1,0:T(8,128)(2,1)S(1)}, bf16[8,512]{1,0:T(8,128)(2,1)S(1)}, u32[]{:S(2)}, u32[]{:S(2)}) %collective-permute-start.5) | collective-permute-done | bytes 8224 | tf_op jit(solution)/shard_map/ppermute | solution.py:11
  18.6 0.6 %collective-permute-done.7 = bf16[8,512]{1,0:T(8,128)(2,1)S(1)} collective-permute-done((bf16[8,512]{1,0:T(8,128)(2,1)S(1)}, bf16[8,512]{1,0:T(8,128)(2,1)S(1)}, u32[]{:S(2)}, u32[]{:S(2)}) %collective-permute-start.7) | collective-permute-done | bytes 8224 | tf_op jit(solution)/shard_map/ppermute | solution.py:11
  19.2 1.2 %collective-permute-done.6 = bf16[8,512]{1,0:T(8,128)(2,1)S(1)} collective-permute-done((bf16[8,512]{1,0:T(8,128)(2,1)S(1)}, bf16[8,512]{1,0:T(8,128)(2,1)S(1)}, u32[]{:S(2)}, u32[]{:S(2)}) %collective-permute-start.6) | collective-permute-done | bytes 8224 | tf_op jit(solution)/shard_map/ppermute | solution.py:11
  20.4 3.7 %collective-permute-start.10 = (bf16[8,512]{1,0:T(8,128)(2,1)S(1)}, bf16[8,512]{1,0:T(8,128)(2,1)S(1)}, u32[]{:S(2)}, u32[]{:S(2)}) collective-permute-start(bf16[8,512]{1,0:T(8,128)(2,1)S(1)} %fusion.7), channel_id=1, source_target_pairs={{0,3},{1,2},{2,1},{3,0},{4,7},{5,6},{6,5},{7,4},{8,11},{9,10},{10,... | collective-permute-start | bytes 24584 | tf_op jit(solution)/shard_map/ppermute | solution.py:11
  24.1 0.0 collective-permute-start.9
  24.1 0.8 %collective-permute-start.8 = (bf16[8,512]{1,0:T(8,128)(2,1)S(1)}, bf16[8,512]{1,0:T(8,128)(2,1)S(1)}, u32[]{:S(2)}, u32[]{:S(2)}) collective-permute-start(bf16[8,512]{1,0:T(8,128)(2,1)S(1)} %fusion.7), channel_id=1, source_target_pairs={{0,1},{1,0},{2,3},{3,2},{4,5},{5,4},{6,7},{7,6},{8,9},{9,8},{10,11... | collective-permute-start | bytes 24584 | tf_op jit(solution)/shard_map/ppermute | solution.py:11
  24.9 1.5 %convolution_convert_fusion = bf16[1024,512]{1,0:T(8,128)(2,1)} fusion(bf16[64,512]{1,0:T(8,128)(2,1)S(1)} %constant_dynamic-update-slice_fusion.2, f32[64,1024]{1,0:T(8,128)S(1)} %get-tuple-element.12, s32[1024]{0:T(1024)S(1)} %copy-done.1, f32[1024]{0:T(1024)S(1)} %fusion, f32[1024]{0:T(1024)S(1)} %get-tuple-element.11, f32[1024]{0:T(1024)S(1)} %copy-done.2, ...), kind=kOutput, calls=%fused_computation.2 | convolution fusion | flops 68091904 | bytes 1392896 | tf_op jit(solution)/shard_map/dot_general | solution.py:104
  26.4 0.0 collective-permute-done.10
  26.4 2.3 %collective-permute-done.9 = bf16[8,512]{1,0:T(8,128)(2,1)S(1)} collective-permute-done((bf16[8,512]{1,0:T(8,128)(2,1)S(1)}, bf16[8,512]{1,0:T(8,128)(2,1)S(1)}, u32[]{:S(2)}, u32[]{:S(2)}) %collective-permute-start.9) | collective-permute-done | bytes 8224 | tf_op jit(solution)/shard_map/ppermute | solution.py:11
  28.6 0.0 collective-permute-done.8
  28.6 1.7 %fusion.8 = f32[512,512]{1,0:T(8,128)} fusion(bf16[8,512]{1,0:T(8,128)(2,1)S(1)} %collective-permute-done.10, bf16[8,512]{1,0:T(8,128)(2,1)S(1)} %collective-permute-done.9, bf16[8,512]{1,0:T(8,128)(2,1)S(1)} %collective-permute-done.8, bf16[8,512]{1,0:T(8,128)(2,1)S(1)} %fusion.7, s32[8]{0:T(128)S(1)} %get-tuple-element.3), kind=kOutput, calls=%fused_computation.19 | convolution fusion | flops 25198592 | bytes 1081376 | tf_op jit(solution)/shard_map/dot_general | solution.py:112
  (15 shorter events, 0.1 us)
Async XLA Ops:
  0.6 11.6 %copy-start = (bf16[1024,512]{1,0:T(8,128)(2,1)S(1)}, bf16[1024,512]{1,0:T(8,128)(2,1)}, u32[]{:S(2)}) copy-start(bf16[1024,512]{1,0:T(8,128)(2,1)} %param.6) | copy-start | bytes 3145732
  3.2 2.1 %collective-permute-start = (bf16[8,512]{1,0:T(8,128)(2,1)S(1)}, bf16[8,512]{1,0:T(8,128)(2,1)S(1)}, u32[]{:S(2)}, u32[]{:S(2)}) collective-permute-start(bf16[8,512]{1,0:T(8,128)(2,1)S(1)} %gather_fusion), channel_id=1, source_target_pairs={{0,4},{4,0},{8,12},{12,8},{16,20},{20,16},{24,28},{28,24},{1,5},{5... | collective-permute-start | bytes 24584 | tf_op jit(solution)/shard_map/ppermute | solution.py:11
  3.8 9.0 %copy-start.1 = (s32[1024]{0:T(1024)S(1)}, s32[1024]{0:T(1024)}, u32[]{:S(2)}) copy-start(s32[1024]{0:T(1024)} %param.10) | copy-start | bytes 12292
  3.8 9.0 %copy-start.2 = (f32[1024]{0:T(1024)S(1)}, f32[1024]{0:T(1024)}, u32[]{:S(2)}) copy-start(f32[1024]{0:T(1024)} %param.11) | copy-start | bytes 12292
  5.2 6.9 %collective-permute-start.3 = (bf16[16,512]{1,0:T(8,128)(2,1)S(1)}, bf16[16,512]{1,0:T(8,128)(2,1)S(1)}, u32[]{:S(2)}, u32[]{:S(2)}) collective-permute-start(bf16[16,512]{1,0:T(8,128)(2,1)S(1)} %get-tuple-element.9), channel_id=1, source_target_pairs={{0,28},{4,24},{8,20},{12,16},{16,12},{20,8},{24,4},{28,0},{1,29},{... | collective-permute-start | bytes 49160 | tf_op jit(solution)/shard_map/ppermute | solution.py:11
  8.9 3.3 %collective-permute-start.2 = (bf16[16,512]{1,0:T(8,128)(2,1)S(1)}, bf16[16,512]{1,0:T(8,128)(2,1)S(1)}, u32[]{:S(2)}, u32[]{:S(2)}) collective-permute-start(bf16[16,512]{1,0:T(8,128)(2,1)S(1)} %get-tuple-element.9), channel_id=1, source_target_pairs={{0,20},{4,16},{8,28},{12,24},{16,4},{20,0},{24,12},{28,8},{1,21},{... | collective-permute-start | bytes 49160 | tf_op jit(solution)/shard_map/ppermute | solution.py:11
  9.0 3.2 %collective-permute-start.1 = (bf16[16,512]{1,0:T(8,128)(2,1)S(1)}, bf16[16,512]{1,0:T(8,128)(2,1)S(1)}, u32[]{:S(2)}, u32[]{:S(2)}) collective-permute-start(bf16[16,512]{1,0:T(8,128)(2,1)S(1)} %get-tuple-element.9), channel_id=1, source_target_pairs={{0,12},{4,8},{8,4},{12,0},{16,28},{20,24},{24,20},{28,16},{1,13},{... | collective-permute-start | bytes 49160 | tf_op jit(solution)/shard_map/ppermute | solution.py:11
  13.1 1.4 %collective-permute-start.4 = (bf16[32,512]{1,0:T(8,128)(2,1)S(1)}, bf16[32,512]{1,0:T(8,128)(2,1)S(1)}, u32[]{:S(2)}, u32[]{:S(2)}) collective-permute-start(bf16[32,512]{1,0:T(8,128)(2,1)S(1)} %pad_maximum_fusion), channel_id=1, source_target_pairs={{0,4},{4,0},{8,12},{12,8},{16,20},{20,16},{24,28},{28,24},{1,5},{5... | collective-permute-start | bytes 98312 | tf_op jit(solution)/shard_map/ppermute | solution.py:11
  14.5 4.0 %collective-permute-start.5 = (bf16[8,512]{1,0:T(8,128)(2,1)S(1)}, bf16[8,512]{1,0:T(8,128)(2,1)S(1)}, u32[]{:S(2)}, u32[]{:S(2)}) collective-permute-start(bf16[8,512]{1,0:T(8,128)(2,1)S(1)} %get-tuple-element.4), channel_id=1, source_target_pairs={{0,28},{4,24},{8,20},{12,16},{16,12},{20,8},{24,4},{28,0},{1,29},{... | collective-permute-start | bytes 24584 | tf_op jit(solution)/shard_map/ppermute | solution.py:11
  16.1 3.1 %collective-permute-start.7 = (bf16[8,512]{1,0:T(8,128)(2,1)S(1)}, bf16[8,512]{1,0:T(8,128)(2,1)S(1)}, u32[]{:S(2)}, u32[]{:S(2)}) collective-permute-start(bf16[8,512]{1,0:T(8,128)(2,1)S(1)} %get-tuple-element.5), channel_id=1, source_target_pairs={{0,12},{4,8},{8,4},{12,0},{16,28},{20,24},{24,20},{28,16},{1,13},{... | collective-permute-start | bytes 24584 | tf_op jit(solution)/shard_map/ppermute | solution.py:11
  17.3 3.1 %collective-permute-start.6 = (bf16[8,512]{1,0:T(8,128)(2,1)S(1)}, bf16[8,512]{1,0:T(8,128)(2,1)S(1)}, u32[]{:S(2)}, u32[]{:S(2)}) collective-permute-start(bf16[8,512]{1,0:T(8,128)(2,1)S(1)} %get-tuple-element.6), channel_id=1, source_target_pairs={{0,20},{4,16},{8,28},{12,24},{16,4},{20,0},{24,12},{28,8},{1,21},{... | collective-permute-start | bytes 24584 | tf_op jit(solution)/shard_map/ppermute | solution.py:11
  20.4 6.0 %collective-permute-start.10 = (bf16[8,512]{1,0:T(8,128)(2,1)S(1)}, bf16[8,512]{1,0:T(8,128)(2,1)S(1)}, u32[]{:S(2)}, u32[]{:S(2)}) collective-permute-start(bf16[8,512]{1,0:T(8,128)(2,1)S(1)} %fusion.7), channel_id=1, source_target_pairs={{0,3},{1,2},{2,1},{3,0},{4,7},{5,6},{6,5},{7,4},{8,11},{9,10},{10,... | collective-permute-start | bytes 24584 | tf_op jit(solution)/shard_map/ppermute | solution.py:11
  24.1 4.5 %collective-permute-start.9 = (bf16[8,512]{1,0:T(8,128)(2,1)S(1)}, bf16[8,512]{1,0:T(8,128)(2,1)S(1)}, u32[]{:S(2)}, u32[]{:S(2)}) collective-permute-start(bf16[8,512]{1,0:T(8,128)(2,1)S(1)} %fusion.7), channel_id=1, source_target_pairs={{0,2},{1,3},{2,0},{3,1},{4,6},{5,7},{6,4},{7,5},{8,10},{9,11},{10,... | collective-permute-start | bytes 24584 | tf_op jit(solution)/shard_map/ppermute | solution.py:11
  24.1 4.5 %collective-permute-start.8 = (bf16[8,512]{1,0:T(8,128)(2,1)S(1)}, bf16[8,512]{1,0:T(8,128)(2,1)S(1)}, u32[]{:S(2)}, u32[]{:S(2)}) collective-permute-start(bf16[8,512]{1,0:T(8,128)(2,1)S(1)} %fusion.7), channel_id=1, source_target_pairs={{0,1},{1,0},{2,3},{3,2},{4,5},{5,4},{6,7},{7,6},{8,9},{9,8},{10,11... | collective-permute-start | bytes 24584 | tf_op jit(solution)/shard_map/ppermute | solution.py:11

commit v2 on v1

--- a/solution.py
+++ b/solution.py
@@ -31,7 +31,7 @@
     for masks in levels_of(size):
         held = sorted(blocks)
         fresh = {}
-        for mask in masks[::-1]:
+        for mask in masks:
             order = sorted(held, key=lambda k: k ^ mask)
             got = exchange(jnp.concatenate([blocks[k] for k in order]), "item", mask)
             for place, piece in zip(order, jnp.split(got, len(order))):
@@ -51,7 +51,7 @@
     for masks, rest in zip(levels, kept[1:]):
         order = sorted(rest)
         got = []
-        for mask in masks[::-1]:
+        for mask in masks:
             out = jnp.concatenate([blocks[k ^ mask] for k in order]).astype(jnp.bfloat16)
             got.append(exchange(out, "item", mask))
         sums = {}
@@ -71,9 +71,9 @@
     while bit < size:
         mine = value.astype(jnp.bfloat16)
         if 2 * bit < size:
+            near = exchange(mine, "dp", bit)
+            mid = exchange(mine, "dp", 2 * bit)
             far = exchange(mine, "dp", 3 * bit)
-            mid = exchange(mine, "dp", 2 * bit)
-            near = exchange(mine, "dp", bit)
             wide = [v.astype(jnp.float32) for v in (mine, near, mid, far)]
             value = (wide[0] + wide[1]) + (wide[2] + wide[3])
             bit *= 4
@@ -84,6 +84,15 @@
     return value
 
 
+def three_pieces(value):
+    pieces = []
+    for _ in range(3):
+        piece = lax.reduce_precision(value, 8, 7)
+        pieces.append(piece.astype(jnp.bfloat16))
+        value = value - piece
+    return pieces
+
+
 def on_device(hidden_states, item_table, cand_local, log_sample, target_slot, loss_weight):
     owners = lax.axis_size("item")
     total_cands = log_sample.shape[0]
@@ -91,11 +100,13 @@
     my_index = lax.axis_index("item")
     my_local = lax.dynamic_slice_in_dim(cand_local, my_index * per_owner, per_owner)
     table_rows = item_table.shape[0]
-    my_rows = item_table[my_local]
+    rows = jnp.arange(table_rows, dtype=jnp.int32)
+    placing = (my_local[:, None] == rows[None, :]).astype(jnp.bfloat16)
+    my_rows = jnp.dot(placing, item_table, preferred_element_type=jnp.float32).astype(jnp.bfloat16)
     cand_rows = gather_rows(my_rows)
     place = jnp.arange(total_cands, dtype=jnp.int32)
     slots = ((place // per_owner) ^ my_index) * per_owner + place % per_owner
-    log_q = log_sample[slots]
+    log_q = jnp.sum(jnp.where(slots[:, None] == place[None, :], log_sample[None, :], 0.0), axis=1)
     logits = jnp.dot(cand_rows, hidden_states.T, preferred_element_type=jnp.float32) - log_q[:, None]
     probs = jax.nn.softmax(logits, axis=0)
     onehot = (target_slot[None, :] == slots[:, None]).astype(jnp.float32)
@@ -106,11 +117,10 @@
     )
     terms = {k: partial[k * per_owner : (k + 1) * per_owner] for k in range(owners)}
     owned = batch_sum(scatter_sum(terms))
-    placing = (my_local[:, None] == jnp.arange(table_rows, dtype=jnp.int32)[None, :]).astype(
-        jnp.float32
-    )
     grad_table = jnp.dot(
-        placing.T, owned, preferred_element_type=jnp.float32, precision=lax.Precision.HIGHEST
+        jnp.concatenate([placing] * 3).T,
+        jnp.concatenate(three_pieces(owned)),
+        preferred_element_type=jnp.float32,
     )
     return (grad_hidden, grad_table)
 

time: 30.5 us -> 29.1 us (0.954)
  local copies, waits for them, and re-layouts: 3.16 us -> 0.85 us
  matrix products: 3.95 us -> 4.89 us
    gather x2 -> x0, local copies, waits for them, and re-layouts: 3.11 us -> none  [the longest x1 1.68 us: on_device(): my_rows = item_table[my_local]]
    dot_general x1 -> x2, matrix products: 1.66 us -> 2.59 us  [the longest x1 1.32 us: on_device(): jnp.dot(jnp.concatenate([placing] * 3).T, jnp.concatenate(three_pieces(ow...]
    select_n x2 -> x0, other arithmetic: 0.83 us -> none  [the longest x1 0.82 us: on_device(): my_rows = item_table[my_local]]
    reduce_sum x0 -> x1, other arithmetic: none -> 0.83 us  [on_device(): jnp.sum(jnp.where(slots[:, None] == place[None, :], log_sample[None, :],...]
    dynamic_slice x0 -> x1, local copies, waits for them, and re-layouts: none -> 0.82 us  [on_device(): lax.dynamic_slice_in_dim(cand_local, my_index * per_owner, per_owner)]
  transfers between devices with their start and end apart: 11 -> 11, of which waited for: 6 -> 5; matrix products, arithmetic and copies ran while one was open for 10% -> 8% of each run, Pallas kernels for 0% -> 0%
where the time goes in v2:
time: 29.1 us; the launch traced here: 28.9 us
  starting transfers between devices  12.5 us (43%)
  waiting for transfers between devices  8.94 us (31%)
  matrix products  4.89 us (17%)
  other arithmetic  1.01 us (3%)
  local copies, waits for them, and re-layouts  0.85 us (3%)
  between operations  0.77 us (3%)
    ppermute x11, starting transfers between devices, exchange(): return lax.ppermute(value, axis, [(i, i ^ mask) for i in range(size)])  12.5 us
    ppermute x11, waiting for transfers between devices, exchange(): return lax.ppermute(value, axis, [(i, i ^ mask) for i in range(size)])  8.94 us
    dot_general x1, matrix products, on_device(): jnp.dot(grad_logits.T, cand_rows, preferred_element_type=jnp.float32)  1.51 us
    dot_general x1, matrix products, on_device(): jnp.dot(jnp.concatenate([placing] * 3).T, jnp.concatenate(three_pieces(ow...  1.32 us
    dot_general x1, matrix products, on_device(): jnp.dot(placing, item_table, preferred_element_type=jnp.float32)  1.27 us
    reduce_sum x1, other arithmetic, on_device(): jnp.sum(jnp.where(slots[:, None] == place[None, :], log_sample[None, :],...  0.83 us
    dynamic_slice x1, local copies, waits for them, and re-layouts, on_device(): lax.dynamic_slice_in_dim(cand_local, my_index * per_owner, per_owner)  0.82 us
  transfers between devices with their start and end apart: 11, of which 5 were waited for; matrix products, arithmetic and copies ran while one was open for 8% of the time, Pallas kernels for 0%

profile of v2, /device:TPU:0, one launch (start us, length us, event | category | flops | bytes accessed | tf_op | source)
XLA Modules:
  0.0 28.9 jit_solution(8531491414019942842)
XLA Ops:
  0.6 0.0 copy-start
  0.7 0.8 %dynamic_slice.3 = s32[8]{0:T(128)S(1)} dynamic-slice(s32[64]{0:T(128)} %param.8, s32[]{:T(128)S(6)} %select_n.27), dynamic_slice_sizes={8} | dynamic-slice | bytes 68 | tf_op jit(solution)/shard_map/dynamic_slice | solution.py:101
  1.5 0.0 copy-start.1
  1.5 0.0 copy-start.2
  1.5 1.3 %constant_dynamic-update-slice_fusion.4 = (bf16[64,512]{1,0:T(8,128)(2,1)S(1)}, bf16[8,512]{1,0:T(8,128)(2,1)S(1)}) fusion(bf16[512,512]{1,0:T(8,128)(2,1)} %param.7, s32[8]{0:T(128)S(1)} %dynamic_slice.3), kind=kOutput, calls=%fused_computation.44 | convolution fusion | flops 4202495 | bytes 540704 | tf_op jit(solution)/shard_map/dot_general | solution.py:105
  2.7 0.5 %collective-permute-start = (bf16[8,512]{1,0:T(8,128)(2,1)S(1)}, bf16[8,512]{1,0:T(8,128)(2,1)S(1)}, u32[]{:S(2)}, u32[]{:S(2)}) collective-permute-start(bf16[8,512]{1,0:T(8,128)(2,1)S(1)} %get-tuple-element.11), channel_id=1, source_target_pairs={{0,4},{4,0},{8,12},{12,8},{16,20},{20,16},{24,28},{28,24},{1,5},{5... | collective-permute-start | bytes 24584 | tf_op jit(solution)/shard_map/ppermute | solution.py:11
  3.3 0.8 %select_reduce_fusion = f32[64]{0:T(128)S(1)} fusion(f32[64]{0:T(128)} %param.9, s32[64]{0:T(128)S(1)} %fusion.21), kind=kLoop, calls=%fused_computation.13 | loop fusion | flops 12224 | bytes 768 | tf_op jit(solution)/shard_map/reduce_sum | solution.py:109
  4.1 0.0 collective-permute-done
  4.1 3.6 %collective-permute-start.3 = (bf16[16,512]{1,0:T(8,128)(2,1)S(1)}, bf16[16,512]{1,0:T(8,128)(2,1)S(1)}, u32[]{:S(2)}, u32[]{:S(2)}) collective-permute-start(bf16[16,512]{1,0:T(8,128)(2,1)S(1)} %pad_maximum_fusion.1), channel_id=1, source_target_pairs={{0,28},{4,24},{8,20},{12,16},{16,12},{20,8},{24,4},{28,0},{1,29},{... | collective-permute-start | bytes 49160 | tf_op jit(solution)/shard_map/ppermute | solution.py:11
  7.7 0.4 %collective-permute-start.2 = (bf16[16,512]{1,0:T(8,128)(2,1)S(1)}, bf16[16,512]{1,0:T(8,128)(2,1)S(1)}, u32[]{:S(2)}, u32[]{:S(2)}) collective-permute-start(bf16[16,512]{1,0:T(8,128)(2,1)S(1)} %pad_maximum_fusion.1), channel_id=1, source_target_pairs={{0,20},{4,16},{8,28},{12,24},{16,4},{20,0},{24,12},{28,8},{1,21},{... | collective-permute-start | bytes 49160 | tf_op jit(solution)/shard_map/ppermute | solution.py:11
  8.1 0.1 collective-permute-start.1
  8.2 3.1 %collective-permute-done.1 = bf16[16,512]{1,0:T(8,128)(2,1)S(1)} collective-permute-done((bf16[16,512]{1,0:T(8,128)(2,1)S(1)}, bf16[16,512]{1,0:T(8,128)(2,1)S(1)}, u32[]{:S(2)}, u32[]{:S(2)}) %collective-permute-start.1) | collective-permute-done | bytes 16416 | tf_op jit(solution)/shard_map/ppermute | solution.py:11
  11.3 0.0 collective-permute-done.2
  11.3 0.0 collective-permute-done.3
  11.3 0.0 copy-done
  11.3 0.5 %fusion.28 = (f32[1024]{0:T(1024)S(1)}, f32[64,1024]{1,0:T(8,128)S(1)}) fusion(f32[64]{0:T(128)S(1)} %select_reduce_fusion, bf16[64,512]{1,0:T(8,128)(2,1)S(1)} %constant_dynamic-update-slice_fusion, bf16[1024,512]{1,0:T(8,128)(2,1)S(1)} %copy-done), kind=kOutput, calls=%fused_computation.57 | convolution fusion | flops 67238912 | bytes 1380608 | tf_op jit(solution)/shard_map/dot_general | solution.py:110
  11.8 0.1 fusion
  11.8 0.0 copy-done.1
  11.8 0.0 copy-done.2
  11.8 0.3 %fusion.29 = (bf16[64,512]{1,0:T(8,128)(2,1)S(1)}, f32[64,512]{1,0:T(8,128)S(1)}) fusion(bf16[1024,512]{1,0:T(8,128)(2,1)S(1)} %copy-done, f32[64,1024]{1,0:T(8,128)S(1)} %get-tuple-element.13, s32[1024]{0:T(1024)S(1)} %copy-done.1, f32[1024]{0:T(1024)S(1)} %fusion, f32[1024]{0:T(1024)S(1)} %get-tuple-element.12, f32[1024]{0:T(1024)S(1)} %copy-done.2, ...), kind=kOutput, calls=%fused_computation.58 | convolution fusion | flops 67600384 | bytes 1523968 | tf_op jit(solution)/shard_map/dot_general | solution.py:114
  12.2 0.3 %collective-permute-start.4 = (bf16[32,512]{1,0:T(8,128)(2,1)S(1)}, bf16[32,512]{1,0:T(8,128)(2,1)S(1)}, u32[]{:S(2)}, u32[]{:S(2)}) collective-permute-start(bf16[32,512]{1,0:T(8,128)(2,1)S(1)} %pad_maximum_fusion), channel_id=1, source_target_pairs={{0,4},{4,0},{8,12},{12,8},{16,20},{20,16},{24,28},{28,24},{1,5},{5... | collective-permute-start | bytes 98312 | tf_op jit(solution)/shard_map/ppermute | solution.py:11
  12.5 0.9 %collective-permute-done.4 = bf16[32,512]{1,0:T(8,128)(2,1)S(1)} collective-permute-done((bf16[32,512]{1,0:T(8,128)(2,1)S(1)}, bf16[32,512]{1,0:T(8,128)(2,1)S(1)}, u32[]{:S(2)}, u32[]{:S(2)}) %collective-permute-start.4) | collective-permute-done | bytes 32800 | tf_op jit(solution)/shard_map/ppermute | solution.py:11
  13.5 0.2 collective-permute-start.5
  13.7 2.5 %collective-permute-start.7 = (bf16[8,512]{1,0:T(8,128)(2,1)S(1)}, bf16[8,512]{1,0:T(8,128)(2,1)S(1)}, u32[]{:S(2)}, u32[]{:S(2)}) collective-permute-start(bf16[8,512]{1,0:T(8,128)(2,1)S(1)} %get-tuple-element.3), channel_id=1, source_target_pairs={{0,28},{4,24},{8,20},{12,16},{16,12},{20,8},{24,4},{28,0},{1,29},{... | collective-permute-start | bytes 24584 | tf_op jit(solution)/shard_map/ppermute | solution.py:11
  16.3 0.4 %collective-permute-start.6 = (bf16[8,512]{1,0:T(8,128)(2,1)S(1)}, bf16[8,512]{1,0:T(8,128)(2,1)S(1)}, u32[]{:S(2)}, u32[]{:S(2)}) collective-permute-start(bf16[8,512]{1,0:T(8,128)(2,1)S(1)} %get-tuple-element.4), channel_id=1, source_target_pairs={{0,20},{4,16},{8,28},{12,24},{16,4},{20,0},{24,12},{28,8},{1,21},{... | collective-permute-start | bytes 24584 | tf_op jit(solution)/shard_map/ppermute | solution.py:11
  16.6 0.1 iota_compare_fusion.1
  16.7 0.0 collective-permute-done.5
  16.7 1.0 %collective-permute-done.7 = bf16[8,512]{1,0:T(8,128)(2,1)S(1)} collective-permute-done((bf16[8,512]{1,0:T(8,128)(2,1)S(1)}, bf16[8,512]{1,0:T(8,128)(2,1)S(1)}, u32[]{:S(2)}, u32[]{:S(2)}) %collective-permute-start.7) | collective-permute-done | bytes 8224 | tf_op jit(solution)/shard_map/ppermute | solution.py:11
  17.7 1.6 %collective-permute-done.6 = bf16[8,512]{1,0:T(8,128)(2,1)S(1)} collective-permute-done((bf16[8,512]{1,0:T(8,128)(2,1)S(1)}, bf16[8,512]{1,0:T(8,128)(2,1)S(1)}, u32[]{:S(2)}, u32[]{:S(2)}) %collective-permute-start.6) | collective-permute-done | bytes 8224 | tf_op jit(solution)/shard_map/ppermute | solution.py:11
  19.4 3.7 %collective-permute-start.10 = (bf16[8,512]{1,0:T(8,128)(2,1)S(1)}, bf16[8,512]{1,0:T(8,128)(2,1)S(1)}, u32[]{:S(2)}, u32[]{:S(2)}) collective-permute-start(bf16[8,512]{1,0:T(8,128)(2,1)S(1)} %fusion.20), channel_id=1, source_target_pairs={{0,3},{1,2},{2,1},{3,0},{4,7},{5,6},{6,5},{7,4},{8,11},{9,10},{10,... | collective-permute-start | bytes 24584 | tf_op jit(solution)/shard_map/ppermute | solution.py:11
  23.0 0.0 collective-permute-start.9
  23.0 0.8 %collective-permute-start.8 = (bf16[8,512]{1,0:T(8,128)(2,1)S(1)}, bf16[8,512]{1,0:T(8,128)(2,1)S(1)}, u32[]{:S(2)}, u32[]{:S(2)}) collective-permute-start(bf16[8,512]{1,0:T(8,128)(2,1)S(1)} %fusion.20), channel_id=1, source_target_pairs={{0,1},{1,0},{2,3},{3,2},{4,5},{5,4},{6,7},{7,6},{8,9},{9,8},{10,11... | collective-permute-start | bytes 24584 | tf_op jit(solution)/shard_map/ppermute | solution.py:11
  23.8 1.5 %convolution_convert_fusion = bf16[1024,512]{1,0:T(8,128)(2,1)} fusion(bf16[64,512]{1,0:T(8,128)(2,1)S(1)} %constant_dynamic-update-slice_fusion, f32[64,1024]{1,0:T(8,128)S(1)} %get-tuple-element.13, s32[1024]{0:T(1024)S(1)} %copy-done.1, f32[1024]{0:T(1024)S(1)} %fusion, f32[1024]{0:T(1024)S(1)} %get-tuple-element.12, f32[1024]{0:T(1024)S(1)} %copy-done.2, ...), kind=kOutput, calls=%fused_computation | convolution fusion | flops 68091904 | bytes 1392896 | tf_op jit(solution)/shard_map/dot_general | solution.py:115
  25.3 0.0 collective-permute-done.10
  25.3 2.3 %collective-permute-done.9 = bf16[8,512]{1,0:T(8,128)(2,1)S(1)} collective-permute-done((bf16[8,512]{1,0:T(8,128)(2,1)S(1)}, bf16[8,512]{1,0:T(8,128)(2,1)S(1)}, u32[]{:S(2)}, u32[]{:S(2)}) %collective-permute-start.9) | collective-permute-done | bytes 8224 | tf_op jit(solution)/shard_map/ppermute | solution.py:11
  27.6 0.0 collective-permute-done.8
  27.6 1.3 %fusion.1 = f32[512,512]{1,0:T(8,128)} fusion(pred[8,512]{1,0:T(8,128)(4,1)S(1)} %iota_compare_fusion.1, bf16[8,512]{1,0:T(8,128)(2,1)S(1)} %get-tuple-element.9, bf16[8,512]{1,0:T(8,128)(2,1)S(1)} %get-tuple-element.8, bf16[8,512]{1,0:T(8,128)(2,1)S(1)} %get-tuple-element.7), kind=kOutput, calls=%fused_computation.6 | convolution fusion | flops 12681216 | bytes 1077248 | tf_op jit(solution)/shard_map/dot_general | solution.py:120
  (12 shorter events, 0.1 us)
Async XLA Ops:
  0.6 10.7 %copy-start = (bf16[1024,512]{1,0:T(8,128)(2,1)S(1)}, bf16[1024,512]{1,0:T(8,128)(2,1)}, u32[]{:S(2)}) copy-start(bf16[1024,512]{1,0:T(8,128)(2,1)} %param.6) | copy-start | bytes 3145732
  1.5 10.3 %copy-start.1 = (s32[1024]{0:T(1024)S(1)}, s32[1024]{0:T(1024)}, u32[]{:S(2)}) copy-start(s32[1024]{0:T(1024)} %param.10) | copy-start | bytes 12292
  1.5 10.4 %copy-start.2 = (f32[1024]{0:T(1024)S(1)}, f32[1024]{0:T(1024)}, u32[]{:S(2)}) copy-start(f32[1024]{0:T(1024)} %param.11) | copy-start | bytes 12292
  2.7 1.4 %collective-permute-start = (bf16[8,512]{1,0:T(8,128)(2,1)S(1)}, bf16[8,512]{1,0:T(8,128)(2,1)S(1)}, u32[]{:S(2)}, u32[]{:S(2)}) collective-permute-start(bf16[8,512]{1,0:T(8,128)(2,1)S(1)} %get-tuple-element.11), channel_id=1, source_target_pairs={{0,4},{4,0},{8,12},{12,8},{16,20},{20,16},{24,28},{28,24},{1,5},{5... | collective-permute-start | bytes 24584 | tf_op jit(solution)/shard_map/ppermute | solution.py:11
  4.1 7.1 %collective-permute-start.3 = (bf16[16,512]{1,0:T(8,128)(2,1)S(1)}, bf16[16,512]{1,0:T(8,128)(2,1)S(1)}, u32[]{:S(2)}, u32[]{:S(2)}) collective-permute-start(bf16[16,512]{1,0:T(8,128)(2,1)S(1)} %pad_maximum_fusion.1), channel_id=1, source_target_pairs={{0,28},{4,24},{8,20},{12,16},{16,12},{20,8},{24,4},{28,0},{1,29},{... | collective-permute-start | bytes 49160 | tf_op jit(solution)/shard_map/ppermute | solution.py:11
  7.7 3.5 %collective-permute-start.2 = (bf16[16,512]{1,0:T(8,128)(2,1)S(1)}, bf16[16,512]{1,0:T(8,128)(2,1)S(1)}, u32[]{:S(2)}, u32[]{:S(2)}) collective-permute-start(bf16[16,512]{1,0:T(8,128)(2,1)S(1)} %pad_maximum_fusion.1), channel_id=1, source_target_pairs={{0,20},{4,16},{8,28},{12,24},{16,4},{20,0},{24,12},{28,8},{1,21},{... | collective-permute-start | bytes 49160 | tf_op jit(solution)/shard_map/ppermute | solution.py:11
  8.1 3.2 %collective-permute-start.1 = (bf16[16,512]{1,0:T(8,128)(2,1)S(1)}, bf16[16,512]{1,0:T(8,128)(2,1)S(1)}, u32[]{:S(2)}, u32[]{:S(2)}) collective-permute-start(bf16[16,512]{1,0:T(8,128)(2,1)S(1)} %pad_maximum_fusion.1), channel_id=1, source_target_pairs={{0,12},{4,8},{8,4},{12,0},{16,28},{20,24},{24,20},{28,16},{1,13},{... | collective-permute-start | bytes 49160 | tf_op jit(solution)/shard_map/ppermute | solution.py:11
  12.2 1.3 %collective-permute-start.4 = (bf16[32,512]{1,0:T(8,128)(2,1)S(1)}, bf16[32,512]{1,0:T(8,128)(2,1)S(1)}, u32[]{:S(2)}, u32[]{:S(2)}) collective-permute-start(bf16[32,512]{1,0:T(8,128)(2,1)S(1)} %pad_maximum_fusion), channel_id=1, source_target_pairs={{0,4},{4,0},{8,12},{12,8},{16,20},{20,16},{24,28},{28,24},{1,5},{5... | collective-permute-start | bytes 98312 | tf_op jit(solution)/shard_map/ppermute | solution.py:11
  13.5 3.2 %collective-permute-start.5 = (bf16[8,512]{1,0:T(8,128)(2,1)S(1)}, bf16[8,512]{1,0:T(8,128)(2,1)S(1)}, u32[]{:S(2)}, u32[]{:S(2)}) collective-permute-start(bf16[8,512]{1,0:T(8,128)(2,1)S(1)} %get-tuple-element.2), channel_id=1, source_target_pairs={{0,12},{4,8},{8,4},{12,0},{16,28},{20,24},{24,20},{28,16},{1,13},{... | collective-permute-start | bytes 24584 | tf_op jit(solution)/shard_map/ppermute | solution.py:11
  13.7 4.0 %collective-permute-start.7 = (bf16[8,512]{1,0:T(8,128)(2,1)S(1)}, bf16[8,512]{1,0:T(8,128)(2,1)S(1)}, u32[]{:S(2)}, u32[]{:S(2)}) collective-permute-start(bf16[8,512]{1,0:T(8,128)(2,1)S(1)} %get-tuple-element.3), channel_id=1, source_target_pairs={{0,28},{4,24},{8,20},{12,16},{16,12},{20,8},{24,4},{28,0},{1,29},{... | collective-permute-start | bytes 24584 | tf_op jit(solution)/shard_map/ppermute | solution.py:11
  16.3 3.1 %collective-permute-start.6 = (bf16[8,512]{1,0:T(8,128)(2,1)S(1)}, bf16[8,512]{1,0:T(8,128)(2,1)S(1)}, u32[]{:S(2)}, u32[]{:S(2)}) collective-permute-start(bf16[8,512]{1,0:T(8,128)(2,1)S(1)} %get-tuple-element.4), channel_id=1, source_target_pairs={{0,20},{4,16},{8,28},{12,24},{16,4},{20,0},{24,12},{28,8},{1,21},{... | collective-permute-start | bytes 24584 | tf_op jit(solution)/shard_map/ppermute | solution.py:11
  19.4 6.0 %collective-permute-start.10 = (bf16[8,512]{1,0:T(8,128)(2,1)S(1)}, bf16[8,512]{1,0:T(8,128)(2,1)S(1)}, u32[]{:S(2)}, u32[]{:S(2)}) collective-permute-start(bf16[8,512]{1,0:T(8,128)(2,1)S(1)} %fusion.20), channel_id=1, source_target_pairs={{0,3},{1,2},{2,1},{3,0},{4,7},{5,6},{6,5},{7,4},{8,11},{9,10},{10,... | collective-permute-start | bytes 24584 | tf_op jit(solution)/shard_map/ppermute | solution.py:11
  23.0 4.5 %collective-permute-start.9 = (bf16[8,512]{1,0:T(8,128)(2,1)S(1)}, bf16[8,512]{1,0:T(8,128)(2,1)S(1)}, u32[]{:S(2)}, u32[]{:S(2)}) collective-permute-start(bf16[8,512]{1,0:T(8,128)(2,1)S(1)} %fusion.20), channel_id=1, source_target_pairs={{0,2},{1,3},{2,0},{3,1},{4,6},{5,7},{6,4},{7,5},{8,10},{9,11},{10,... | collective-permute-start | bytes 24584 | tf_op jit(solution)/shard_map/ppermute | solution.py:11
  23.0 4.5 %collective-permute-start.8 = (bf16[8,512]{1,0:T(8,128)(2,1)S(1)}, bf16[8,512]{1,0:T(8,128)(2,1)S(1)}, u32[]{:S(2)}, u32[]{:S(2)}) collective-permute-start(bf16[8,512]{1,0:T(8,128)(2,1)S(1)} %fusion.20), channel_id=1, source_target_pairs={{0,1},{1,0},{2,3},{3,2},{4,5},{5,4},{6,7},{7,6},{8,9},{9,8},{10,11... | collective-permute-start | bytes 24584 | tf_op jit(solution)/shard_map/ppermute | solution.py:11
